TPU v7x, 256 devices: a whole 4x4x8 slice. The times are simulated.
256 devices in a mesh: pairs: 64 (over y, z, core), orb: 4 (over x).
Axes of the slice: x: 4, y: 4, z: 8, core: 2. Of those that a mesh axis runs over, the one named last changes fastest.
Arguments:
- amplitudes: float32 [1024, 128, 128], P(('pairs', 'orb')), may hold values from -4 to 4
- integrals: bfloat16 [1024, 128, 128], P(('pairs', 'orb')), may hold values from -6 to 6
- energies: float32 [1024, 128], P(('pairs', 'orb')), may hold values from 0.5 to 4
- intersections: bfloat16 [1024, 16, 128, 128], P(('pairs', 'orb')), may hold values from -0.5 to 0.5
- couplings: float32 [1024, 16], P(('pairs', 'orb')), may hold values from -2 to 2
- projector: float32 [1024, 128], P(('pairs', 'orb')), may hold values from -0.5 to 0.5
- pair_orbitals: int32 [1024, 2], P(('pairs', 'orb')), may hold values from 0 to 31
- coupled: int32 [1024, 16], replicated, may hold values from 0 to 1023, as said below
- pair_slot: int32 [1024], replicated, may hold values from 0 to 1023, as said below
Outputs:
- final_amplitudes: float32 [1024, 128, 128], P(('pairs', 'orb'))
- residual: float32 [1024, 128, 128], P(('pairs', 'orb'))
Inputs may be any that keep to these rules, and one draw needn't show every extreme that they name: `coupled`: each row holds 16 different pair ids, never the id of the pair held in that row's slot. The rows of one device name at most 1 different pairs held by the devices of any one pairs index, and exactly 1 held by the devices of the next pairs index. `pair_slot`: A permutation of the pair ids.
All inputs are finite; a program needn't handle non-finite values.
Results may differ from a plain program's by a relative error of at most 0.00037.
Values may be sent and summed in bfloat16 or wider, within the bound.
A program may use at most 64 MiB of HBM per device.

v0:
```python
import jax
import jax.numpy as jnp
from jax import lax
from jax.sharding import PartitionSpec as P

PAIRS_ORB = 32
ITERS = 2


def body(
    amplitudes,
    integrals,
    energies,
    intersections,
    couplings,
    projector,
    pair_orbitals,
    coupled,
    pair_slot,
):
    highest = lax.Precision.HIGHEST
    pair_count = lax.axis_size("pairs")
    orb_count = lax.axis_size("orb")
    devices = pair_count * orb_count
    per_device = amplitudes.shape[0]
    width = amplitudes.shape[1]
    total = coupled.shape[0]
    capacity = 1 + coupled.shape[1] // pair_count
    group = orb_count * per_device
    orbitals = total // PAIRS_ORB
    pair_idx = lax.axis_index("pairs")
    orb_idx = lax.axis_index("orb")
    device_id = pair_idx * orb_count + orb_idx
    targets = pair_slot[coupled]
    row_owner = jnp.broadcast_to(
        (jnp.arange(total, dtype=jnp.int32) // per_device)[:, None], targets.shape
    )
    needed = jnp.zeros((devices, total), jnp.int32).at[row_owner, targets].set(1)
    mine = lax.dynamic_slice_in_dim(needed, device_id, 1, 0)[0].reshape(pair_count, group)
    ranks = (jnp.cumsum(mine, axis=1) - 1).reshape(total)
    own_targets = lax.dynamic_slice_in_dim(targets, device_id * per_device, per_device, 0)
    slot_ids = jnp.arange(capacity, dtype=jnp.int32)
    group_cols = lax.dynamic_slice_in_dim(needed, pair_idx * group, group, 1)
    group_rank = jnp.cumsum(group_cols, axis=1) - 1
    entry_pos = own_targets // group * capacity + ranks[own_targets]
    dest_cols = group_cols.reshape(pair_count, orb_count, group)
    dest_cols = lax.dynamic_slice_in_dim(dest_cols, orb_idx, 1, 1)[:, 0]
    dest_rank = group_rank.reshape(pair_count, orb_count, group)
    dest_rank = lax.dynamic_slice_in_dim(dest_rank, orb_idx, 1, 1)[:, 0]
    select = (
        (dest_cols == 1)[:, None, :] & (dest_rank[:, None, :] == slot_ids[None, :, None])
    ).astype(jnp.bfloat16)
    orbital_ids = jnp.arange(orbitals, dtype=jnp.int32)
    first_hot = (pair_orbitals[:, 0:1] == orbital_ids[None, :]).astype(jnp.float32)
    second_hot = (pair_orbitals[:, 1:2] == orbital_ids[None, :]).astype(jnp.float32)
    denom = energies[:, :, None] + energies[:, None, :]
    state = amplitudes
    residual = amplitudes
    for step in range(ITERS):
        blocks = state.astype(jnp.bfloat16)
        group_blocks = lax.all_gather(blocks, "orb", axis=0, tiled=True)
        outgoing = jnp.einsum(
            "pcj,jxy->pcxy", select, group_blocks, preferred_element_type=jnp.float32
        )
        outgoing = outgoing.astype(jnp.bfloat16)
        arrived = lax.all_to_all(outgoing, "pairs", split_axis=0, concat_axis=0, tiled=True)
        arrived = arrived.reshape(pair_count * capacity, width, width)
        fetched = arrived[entry_pos]
        lifted = jnp.einsum(
            "pkab,pkbc->pkac", intersections, fetched, preferred_element_type=jnp.float32
        )
        scaled = (couplings[:, :, None, None] * lifted).astype(jnp.bfloat16)
        coupling = jnp.einsum(
            "pkac,pkdc->pad", scaled, intersections, preferred_element_type=jnp.float32
        )
        projected = jnp.einsum("pab,pb->pa", state, projector, precision=highest)
        partial_sum = jnp.dot(first_hot.T, projected, precision=highest) + jnp.dot(
            second_hot.T, projected, precision=highest
        )
        summed = lax.psum(partial_sum, ("pairs", "orb"))
        left = jnp.dot(first_hot, summed, precision=highest)
        right = jnp.dot(second_hot, summed, precision=highest)
        residual = (
            integrals.astype(jnp.float32)
            + energies[:, :, None] * state
            + state * energies[:, None, :]
            - coupling
            + left[:, :, None] * projector[:, None, :]
            + projector[:, :, None] * right[:, None, :]
        )
        state = state - residual / denom
    return (state, residual)


def solution(mesh):
    return jax.shard_map(
        body,
        mesh=mesh,
        in_specs=(
            P(("pairs", "orb"), None, None),
            P(("pairs", "orb"), None, None),
            P(("pairs", "orb"), None),
            P(("pairs", "orb"), None, None, None),
            P(("pairs", "orb"), None),
            P(("pairs", "orb"), None),
            P(("pairs", "orb"), None),
            P(),
            P(),
        ),
        out_specs=(P(("pairs", "orb"), None, None), P(("pairs", "orb"), None, None)),
        check_vma=False,
    )
```

profile of v0, /device:TPU:1, one launch (start us, length us, event | category | flops | bytes accessed | tf_op | source)
XLA Modules:
  0.0 392.0 jit_solution(17940552267861765877)
XLA Ops:
  0.6 0.0 copy-start
  0.7 0.6 add_select_fusion
  1.3 0.6 broadcast_compare_fusion
  1.9 0.8 compare_select_fusion.1
  2.7 0.2 copy.38
  2.9 0.2 reshape.137
  3.1 65.3 %gather_fusion = s32[16384]{0:T(1024)S(1)} fusion(s32[1024]{0:T(1024)S(1)} %copy-done.1, s32[16384]{0:T(1024)S(1)} %broadcast_clamp_fusion), kind=kCustom, calls=%fused_computation | custom fusion | bytes 196608 | tf_op jit(solution)/shard_map/gather | solution.py:34
  68.4 0.0 copy-start.3
  68.4 0.0 copy-start.4
  68.4 0.0 copy-start.9
  68.4 0.0 copy-start.8
  68.5 0.2 gather.15
  68.6 0.1 compare_select_fusion
  68.7 0.2 copy.39
  68.9 0.2 copy-done.3
  69.1 0.0 copy-done.4
  69.1 0.0 copy-done.6
  69.1 0.1 multiply_reduce_fusion
  69.2 0.1 and_reduce_fusion
  69.3 0.2 copy.40
  69.5 0.2 reshape.167
  69.7 0.0 copy-start.2
  69.8 0.6 broadcast.186
  70.4 60.8 %scatter_custom_fusion = s32[262144]{0:T(1024)S(1)} fusion(s32[16384]{0:T(1024)S(1)} %reshape.167, s32[16384]{0:T(1024)} %broadcast.186, s32[]{:T(128)} %constant.52.clone.1), kind=kCustom, calls=%fused_computation.28 | custom fusion | bytes 1049088
  131.2 1.1 reshape.134
  132.3 1.0 constant_dynamic-slice_fusion
  133.4 0.7 reduce_window_sum.22
  134.1 12.3 %all_gather.6 = bf16[16,128,128]{2,1,0:T(8,128)(2,1)S(1)} all-gather(bf16[4,128,128]{2,1,0:T(8,128)(2,1)S(1)} %convert_element_type.38), channel_id=1, replica_groups=mesh['pairs'=64,'orb'=4] {'orb'}, dimensions={0}, use_global_device_ids=true | all-gather | bytes 655360 | tf_op jit(solution)/shard_map/all_gather | solution.py:61
  146.4 0.7 convert_bitcast_fusion.1
  147.1 2.6 copy.45
  149.8 14.2 %all-to-all-start = ((bf16[64,1,128,128]{3,2,1,0:T(8,128)(2,1)}), bf16[64,1,128,128]{3,2,1,0:T(8,128)(2,1)}, u32[]{:S(2)}, u32[]{:S(2)}) async-start(bf16[64,1,128,128]{3,2,1,0:T(8,128)(2,1)} %copy.45), calls=%async_computation | async-start | bytes 4194304 | tf_op jit(solution)/shard_map/all_to_all | solution.py:66
  164.0 0.0 copy-start.7
  164.0 0.0 copy-start.5
  164.0 0.2 reshape.136
  164.2 0.8 dynamic-slice_reduce_fusion
  165.0 0.1 reshape_squeeze.3
  165.1 0.2 reduce_window_sum.23
  165.2 0.1 sub.37
  165.3 0.1 reshape.145
  165.4 0.7 gather_fusion.1
  166.2 0.1 reshape.144
  166.3 0.1 reshape.153
  166.4 0.5 fusion.65
  166.9 0.3 fusion.54
  167.2 0.3 convolution_add_fusion.1
  167.4 89.2 %psum.14 = f32[32,128]{1,0:T(8,128)S(1)} all-reduce(f32[32,128]{1,0:T(8,128)S(1)} %convolution_add_fusion.1), channel_id=1, replica_groups=mesh['pairs'=64,'orb'=4] {'pairs','orb'}, use_global_device_ids=true, to_apply=%region_3.4 | all-reduce | flops 4096 | bytes 32768 | tf_op jit(solution)/shard_map/psum | solution.py:80
  256.7 0.2 fusion.53
  256.9 0.2 fusion.50
  257.0 0.0 copy-start.11
  257.1 0.0 copy-start.12
  257.1 3.7 gather_fusion.2
  260.8 3.8 fusion.64
  264.6 11.4 %all_gather.7 = bf16[16,128,128]{2,1,0:T(8,128)(2,1)S(1)} all-gather(bf16[4,128,128]{2,1,0:T(8,128)(2,1)S(1)} %get-tuple-element.4), channel_id=1, replica_groups=mesh['pairs'=64,'orb'=4] {'orb'}, dimensions={0}, use_global_device_ids=true | all-gather | bytes 655360 | tf_op jit(solution)/shard_map/all_gather | solution.py:61
  276.1 0.7 convert_bitcast_fusion
  276.8 2.6 copy.50
  279.4 11.7 %all-to-all-start.1 = ((bf16[64,1,128,128]{3,2,1,0:T(8,128)(2,1)}), bf16[64,1,128,128]{3,2,1,0:T(8,128)(2,1)}, u32[]{:S(2)}, u32[]{:S(2)}) async-start(bf16[64,1,128,128]{3,2,1,0:T(8,128)(2,1)} %copy.50), calls=%async_computation.1 | async-start | bytes 4194304 | tf_op jit(solution)/shard_map/all_to_all | solution.py:66
  291.1 0.5 fusion.66
  291.6 0.3 fusion.52
  291.9 0.3 convolution_add_fusion
  292.2 91.1 %psum.15 = f32[32,128]{1,0:T(8,128)S(1)} all-reduce(f32[32,128]{1,0:T(8,128)S(1)} %convolution_add_fusion), channel_id=1, replica_groups=mesh['pairs'=64,'orb'=4] {'pairs','orb'}, use_global_device_ids=true, to_apply=%region_4.5 | all-reduce | flops 4096 | bytes 32768 | tf_op jit(solution)/shard_map/psum | solution.py:80
  383.3 0.2 fusion.51
  383.5 0.2 fusion.49
  383.7 3.7 gather_fusion.3
  387.4 4.6 %fusion.40 = (f32[4,128,128]{2,1,0:T(8,128)}, f32[4,128,128]{2,1,0:T(8,128)}) fusion(f32[4,128,128]{2,1,0:T(8,128)S(1)} %get-tuple-element.5, f32[4,128]{1,0:T(4,128)S(1)} %copy-done.12, f32[4,128]{1,0:T(4,128)S(1)} %fusion.49, f32[4,128]{1,0:T(4,128)S(1)} %copy-done.5, f32[4,128]{1,0:T(4,128)S(1)} %fusion.51, bf16[4,16,128,128]{3,2,1,0:T(8,128)(2,1)S(1)} %copy-done, ...), kind=kOutput, calls=%fused_computation.35 | convolution fusion | flops 539820032 | bytes 5120256 | tf_op jit(solution)/shard_map/pkac,pkdc->pad/dot_general | solution.py:73
  (27 shorter events, 0.2 us)
Async XLA Ops:
  0.6 260.2 %copy-start = (bf16[4,16,128,128]{3,2,1,0:T(8,128)(2,1)S(1)}, bf16[4,16,128,128]{3,2,1,0:T(8,128)(2,1)}, u32[]{:S(2)}) copy-start(bf16[4,16,128,128]{3,2,1,0:T(8,128)(2,1)} %param.12) | copy-start | bytes 6291460
  0.6 2.5 copy-start.1
  68.4 0.7 copy-start.3
  68.4 0.7 copy-start.4
  68.4 0.7 copy-start.6
  68.4 0.7 copy-start.9
  68.4 0.8 copy-start.8
  69.7 64.4 %copy-start.2 = (f32[4,128,128]{2,1,0:T(8,128)S(1)}, f32[4,128,128]{2,1,0:T(8,128)}, u32[]{:S(2)}) copy-start(f32[4,128,128]{2,1,0:T(8,128)} %param.9) | copy-start | bytes 786436
  149.8 107.3 %all-to-all-start = ((bf16[64,1,128,128]{3,2,1,0:T(8,128)(2,1)}), bf16[64,1,128,128]{3,2,1,0:T(8,128)(2,1)}, u32[]{:S(2)}, u32[]{:S(2)}) async-start(bf16[64,1,128,128]{3,2,1,0:T(8,128)(2,1)} %copy.45), calls=%async_computation | async-start | bytes 4194304 | tf_op jit(solution)/shard_map/all_to_all | solution.py:66
  164.0 2.4 copy-start.7
  164.0 2.4 copy-start.5
  257.0 3.8 copy-start.10
  257.0 3.8 copy-start.11
  257.1 3.8 copy-start.12
  279.4 104.3 %all-to-all-start.1 = ((bf16[64,1,128,128]{3,2,1,0:T(8,128)(2,1)}), bf16[64,1,128,128]{3,2,1,0:T(8,128)(2,1)}, u32[]{:S(2)}, u32[]{:S(2)}) async-start(bf16[64,1,128,128]{3,2,1,0:T(8,128)(2,1)} %copy.50), calls=%async_computation.1 | async-start | bytes 4194304 | tf_op jit(solution)/shard_map/all_to_all | solution.py:66
where the time goes:
time: 393 us; the launch traced here: 392 us
  blocking collectives  204 us (52%)
  local copies, waits for them, and re-layouts  145 us (37%)
  starting transfers between devices  25.9 us (7%)
  matrix products  12.6 us (3%)
    psum x2, blocking collectives, body(): summed = lax.psum(partial_sum, ('pairs', 'orb'))  180 us
    gather x3, local copies, waits for them, and re-layouts, body(): targets = pair_slot[coupled]  65.6 us
    unnamed x30, local copies, waits for them, and re-layouts  62.1 us
    all_to_all x2, starting transfers between devices, body(): lax.all_to_all(outgoing, 'pairs', split_axis=0, concat_axis=0, tiled=True)  25.9 us
    all_gather x2, blocking collectives, body(): group_blocks = lax.all_gather(blocks, 'orb', axis=0, tiled=True)  23.7 us
    dot_general x2, matrix products, body(): jnp.einsum('pkac,pkdc->pad', scaled, intersections, preferred_element_typ...  8.38 us
  transfers between devices with their start and end apart: 2, of which 0 were waited for; matrix products, arithmetic and copies ran while one was open for 1% of the time, Pallas kernels for 0%

commit v1 on v0

--- a/solution.py
+++ b/solution.py
@@ -77,7 +77,7 @@
         partial_sum = jnp.dot(first_hot.T, projected, precision=highest) + jnp.dot(
             second_hot.T, projected, precision=highest
         )
-        summed = lax.psum(partial_sum, ("pairs", "orb"))
+        summed = lax.psum(lax.psum(partial_sum, "pairs"), "orb")
         left = jnp.dot(first_hot, summed, precision=highest)
         right = jnp.dot(second_hot, summed, precision=highest)
         residual = (

time: 393 us -> 807 us (2.05)
  blocking collectives: 204 us -> 606 us
    psum x2 -> x4, blocking collectives: 180 us -> 584 us  [body(): summed = lax.psum(lax.psum(partial_sum, 'pairs'), 'orb')]
where the time goes in v1:
time: 807 us; the launch traced here: 799 us
  blocking collectives  606 us (75%)
  local copies, waits for them, and re-layouts  145 us (18%)
  starting transfers between devices  31.2 us (4%)
  matrix products  12.6 us (2%)
    psum x4, blocking collectives, body(): summed = lax.psum(lax.psum(partial_sum, 'pairs'), 'orb')  584 us
    gather x3, local copies, waits for them, and re-layouts, body(): targets = pair_slot[coupled]  65.6 us
    unnamed x30, local copies, waits for them, and re-layouts  62.1 us
    all_to_all x2, starting transfers between devices, body(): lax.all_to_all(outgoing, 'pairs', split_axis=0, concat_axis=0, tiled=True)  31.2 us
    all_gather x2, blocking collectives, body(): group_blocks = lax.all_gather(blocks, 'orb', axis=0, tiled=True)  22.4 us
  transfers between devices with their start and end apart: 2, of which 0 were waited for; matrix products, arithmetic and copies ran while one was open for 1% of the time, Pallas kernels for 0%

profile of v1, /device:TPU:1, one launch (start us, length us, event | category | flops | bytes accessed | tf_op | source)
XLA Modules:
  0.0 799.4 jit_solution(15587189230968977783)
XLA Ops:
  0.6 0.0 copy-start
  0.7 0.6 add_select_fusion
  1.3 0.6 broadcast_compare_fusion
  1.9 0.8 compare_select_fusion.1
  2.7 0.2 copy.38
  2.9 0.2 reshape.137
  3.1 65.3 %gather_fusion = s32[16384]{0:T(1024)S(1)} fusion(s32[1024]{0:T(1024)S(1)} %copy-done.1, s32[16384]{0:T(1024)S(1)} %broadcast_clamp_fusion), kind=kCustom, calls=%fused_computation | custom fusion | bytes 196608 | tf_op jit(solution)/shard_map/gather | solution.py:34
  68.4 0.0 copy-start.3
  68.4 0.0 copy-start.9
  68.4 0.0 copy-start.8
  68.5 0.2 gather.15
  68.6 0.1 compare_select_fusion
  68.7 0.2 copy.39
  68.9 0.2 copy-done.3
  69.1 0.0 copy-done.4
  69.1 0.0 copy-done.6
  69.1 0.1 multiply_reduce_fusion
  69.2 0.1 and_reduce_fusion
  69.3 0.2 copy.40
  69.5 0.2 reshape.167
  69.7 0.0 copy-start.2
  69.8 0.6 broadcast.186
  70.4 60.8 %scatter_custom_fusion = s32[262144]{0:T(1024)S(1)} fusion(s32[16384]{0:T(1024)S(1)} %reshape.167, s32[16384]{0:T(1024)} %broadcast.186, s32[]{:T(128)} %constant.52.clone.1), kind=kCustom, calls=%fused_computation.28 | custom fusion | bytes 1049088
  131.2 1.1 reshape.134
  132.3 1.0 constant_dynamic-slice_fusion
  133.4 0.7 reduce_window_sum.22
  134.1 12.3 %all_gather.6 = bf16[16,128,128]{2,1,0:T(8,128)(2,1)S(1)} all-gather(bf16[4,128,128]{2,1,0:T(8,128)(2,1)S(1)} %convert_element_type.38), channel_id=1, replica_groups=mesh['pairs'=64,'orb'=4] {'orb'}, dimensions={0}, use_global_device_ids=true | all-gather | bytes 655360 | tf_op jit(solution)/shard_map/all_gather | solution.py:61
  146.4 0.7 convert_bitcast_fusion.1
  147.1 2.6 copy.45
  149.8 14.2 %all-to-all-start = ((bf16[64,1,128,128]{3,2,1,0:T(8,128)(2,1)}), bf16[64,1,128,128]{3,2,1,0:T(8,128)(2,1)}, u32[]{:S(2)}, u32[]{:S(2)}) async-start(bf16[64,1,128,128]{3,2,1,0:T(8,128)(2,1)} %copy.45), calls=%async_computation | async-start | bytes 4194304 | tf_op jit(solution)/shard_map/all_to_all | solution.py:66
  164.0 0.0 copy-start.7
  164.0 0.0 copy-start.5
  164.0 0.2 reshape.136
  164.2 0.8 dynamic-slice_reduce_fusion
  165.0 0.1 reshape_squeeze.3
  165.1 0.2 reduce_window_sum.23
  165.2 0.1 sub.37
  165.3 0.1 reshape.145
  165.4 0.7 gather_fusion.1
  166.2 0.1 reshape.144
  166.3 0.1 reshape.153
  166.4 0.5 fusion.65
  166.9 0.3 fusion.54
  167.2 0.3 convolution_add_fusion.1
  167.4 278.5 %psum.28 = f32[32,128]{1,0:T(8,128)S(1)} all-reduce(f32[32,128]{1,0:T(8,128)S(1)} %convolution_add_fusion.1), channel_id=1, replica_groups=mesh['pairs'=64,'orb'=4] {'pairs'}, use_global_device_ids=true, to_apply=%region_3.4 | all-reduce | flops 4096 | bytes 32768 | tf_op jit(solution)/shard_map/psum | solution.py:80
  445.9 13.6 %psum.29 = f32[32,128]{1,0:T(8,128)S(1)} all-reduce(f32[32,128]{1,0:T(8,128)S(1)} %psum.28), channel_id=1, replica_groups=mesh['pairs'=64,'orb'=4] {'orb'}, use_global_device_ids=true, to_apply=%region_4.5 | all-reduce | flops 4096 | bytes 32768 | tf_op jit(solution)/shard_map/psum | solution.py:80
  459.6 0.2 fusion.53
  459.7 0.2 fusion.50
  459.9 0.0 copy-start.11
  460.0 3.7 gather_fusion.2
  463.7 3.8 fusion.64
  467.5 10.1 %all_gather.7 = bf16[16,128,128]{2,1,0:T(8,128)(2,1)S(1)} all-gather(bf16[4,128,128]{2,1,0:T(8,128)(2,1)S(1)} %get-tuple-element.4), channel_id=1, replica_groups=mesh['pairs'=64,'orb'=4] {'orb'}, dimensions={0}, use_global_device_ids=true | all-gather | bytes 655360 | tf_op jit(solution)/shard_map/all_gather | solution.py:61
  477.6 0.7 convert_bitcast_fusion
  478.3 2.6 copy.50
  480.9 16.9 %all-to-all-start.1 = ((bf16[64,1,128,128]{3,2,1,0:T(8,128)(2,1)}), bf16[64,1,128,128]{3,2,1,0:T(8,128)(2,1)}, u32[]{:S(2)}, u32[]{:S(2)}) async-start(bf16[64,1,128,128]{3,2,1,0:T(8,128)(2,1)} %copy.50), calls=%async_computation.1 | async-start | bytes 4194304 | tf_op jit(solution)/shard_map/all_to_all | solution.py:66
  497.9 0.5 fusion.66
  498.4 0.3 fusion.52
  498.7 0.3 convolution_add_fusion
  499.0 280.9 %psum.30 = f32[32,128]{1,0:T(8,128)S(1)} all-reduce(f32[32,128]{1,0:T(8,128)S(1)} %convolution_add_fusion), channel_id=1, replica_groups=mesh['pairs'=64,'orb'=4] {'pairs'}, use_global_device_ids=true, to_apply=%region_5.6 | all-reduce | flops 4096 | bytes 32768 | tf_op jit(solution)/shard_map/psum | solution.py:80
  779.9 10.8 %psum.31 = f32[32,128]{1,0:T(8,128)S(1)} all-reduce(f32[32,128]{1,0:T(8,128)S(1)} %psum.30), channel_id=1, replica_groups=mesh['pairs'=64,'orb'=4] {'orb'}, use_global_device_ids=true, to_apply=%region_6.7 | all-reduce | flops 4096 | bytes 32768 | tf_op jit(solution)/shard_map/psum | solution.py:80
  790.7 0.2 fusion.51
  790.9 0.2 fusion.49
  791.1 3.7 gather_fusion.3
  794.8 4.6 fusion.40
  (29 shorter events, 0.2 us)
Async XLA Ops:
  0.6 463.1 %copy-start = (bf16[4,16,128,128]{3,2,1,0:T(8,128)(2,1)S(1)}, bf16[4,16,128,128]{3,2,1,0:T(8,128)(2,1)}, u32[]{:S(2)}) copy-start(bf16[4,16,128,128]{3,2,1,0:T(8,128)(2,1)} %param.12) | copy-start | bytes 6291460
  0.6 2.5 copy-start.1
  68.4 0.7 copy-start.3
  68.4 0.7 copy-start.4
  68.4 0.7 copy-start.6
  68.4 0.7 copy-start.9
  68.4 0.8 copy-start.8
  69.7 64.4 %copy-start.2 = (f32[4,128,128]{2,1,0:T(8,128)S(1)}, f32[4,128,128]{2,1,0:T(8,128)}, u32[]{:S(2)}) copy-start(f32[4,128,128]{2,1,0:T(8,128)} %param.9) | copy-start | bytes 786436
  149.8 310.2 %all-to-all-start = ((bf16[64,1,128,128]{3,2,1,0:T(8,128)(2,1)}), bf16[64,1,128,128]{3,2,1,0:T(8,128)(2,1)}, u32[]{:S(2)}, u32[]{:S(2)}) async-start(bf16[64,1,128,128]{3,2,1,0:T(8,128)(2,1)} %copy.45), calls=%async_computation | async-start | bytes 4194304 | tf_op jit(solution)/shard_map/all_to_all | solution.py:66
  164.0 2.4 copy-start.7
  164.0 2.4 copy-start.5
  459.9 3.8 copy-start.10
  459.9 3.8 copy-start.11
  459.9 3.8 copy-start.12
  480.9 310.1 %all-to-all-start.1 = ((bf16[64,1,128,128]{3,2,1,0:T(8,128)(2,1)}), bf16[64,1,128,128]{3,2,1,0:T(8,128)(2,1)}, u32[]{:S(2)}, u32[]{:S(2)}) async-start(bf16[64,1,128,128]{3,2,1,0:T(8,128)(2,1)} %copy.50), calls=%async_computation.1 | async-start | bytes 4194304 | tf_op jit(solution)/shard_map/all_to_all | solution.py:66
